TPU v7x, 32 devices: a whole 2x2x4 slice. The times are simulated.
32 devices in a mesh: parts: 2 (over y), seq: 8 (over z, core), rep: 2 (over x), head: 1.
Axes of the slice: x: 2, y: 2, z: 4, core: 2. Of those that a mesh axis runs over, the one named last changes fastest.
Arguments:
- activations: bfloat16 [4, 1024, 2048], P(('parts', 'rep'), 'seq', 'head'), parts along dimension 0, may hold values from -6 to 6
- value_weight: bfloat16 [2048, 2048], P(('seq', 'rep'), 'head'), may hold values from -0.125 to 0.125
- query_in: bfloat16 [4, 1024, 2048], P(('parts', 'rep'), 'seq', 'head'), parts along dimension 0, may hold values from -6 to 6
- key_in: bfloat16 [4, 1024, 2048], P(('parts', 'rep'), 'seq', 'head'), parts along dimension 0, may hold values from -6 to 6
- grad_out: bfloat16 [4, 1024, 2048], P(('parts', 'rep'), 'seq', 'head'), parts along dimension 0, may hold values from -6 to 6
- conv_kernel: float32 [3, 4, 2048], P(None, None, 'head'), may hold values from -3 to 3
- log_gate: float32 [4, 16, 1024], P(('parts', 'rep'), 'head', 'seq'), parts along dimension 0, as said below
Outputs:
- attn_out: bfloat16 [4, 1024, 2048], P(('parts', 'rep'), 'seq', 'head'), parts along dimension 0
- grad_query: bfloat16 [4, 1024, 2048], P(('parts', 'rep'), 'seq', 'head'), parts along dimension 0
- grad_key: bfloat16 [4, 1024, 2048], P(('parts', 'rep'), 'seq', 'head'), parts along dimension 0
- grad_x: bfloat16 [4, 1024, 2048], P(('parts', 'rep'), 'seq', 'head'), parts along dimension 0
- grad_w: float32 [4096, 2048], P(('parts', 'seq', 'rep'), 'head'), parts along dimension 0
- grad_conv: float32 [6, 4, 2048], P('parts', None, 'head'), parts along dimension 0
There are 2 independent parts, one for each index of `parts`. A program takes and returns all parts, laid end to end along the dimension named above; an argument that names none is the same for every part. Nothing has to cross between parts.
Inputs may be any that keep to these rules, and one draw needn't show every extreme that they name: `log_gate`: every entry is below zero.
All inputs are finite; a program needn't handle non-finite values.
Results may differ from a plain program's by a relative error of at most 0.015.
Values may be sent and summed in bfloat16 or wider, within the bound.
A program may use at most 128 MiB of HBM per device.

v0:
```python
import math
import jax
import jax.numpy as jnp
from jax import lax
from jax.sharding import PartitionSpec as P

EPSILON = 1e-06


def shifted(block, axis, distance):
    devices = range(lax.axis_size(axis))
    route = [(i - distance, i) for i in devices if i - distance in devices]
    return lax.ppermute(block, axis, route)


def prefix(part, axis, combine, identity, reverse):
    count = lax.axis_size(axis)
    place = lax.axis_index(axis)
    ahead = count - 1 - place if reverse else place
    gathered = jax.tree.map(lambda a: lax.all_gather(a, axis), part)
    state = jax.tree.map(lambda a, e: jnp.zeros_like(a) + jnp.asarray(e, a.dtype), part, identity)

    def one(step, state):
        source = count - 1 - step if reverse else step
        return combine(
            state, jax.tree.map(lambda a: lax.dynamic_index_in_dim(a, source, 0, False), gathered)
        )

    return lax.fori_loop(0, ahead, one, state)


def carried_in(value, axis, combine, identity, reverse):
    length, mine = (lax.axis_size(axis), lax.axis_index(axis))
    everything = jax.tree.map(
        lambda part, kind: lax.all_gather(part.astype(kind), axis),
        value,
        (jnp.bfloat16, jnp.bfloat16),
    )
    start = jax.tree.map(
        lambda part, zero: jnp.broadcast_to(jnp.asarray(zero, part.dtype), part.shape),
        value,
        identity,
    )

    def step(k, before):
        at = length - 1 - k if reverse else k
        reached = at > mine if reverse else at < mine
        new = combine(
            before, jax.tree.map(lambda part, own: part[at].astype(own.dtype), everything, value)
        )
        return jax.tree.map(lambda a, b: jnp.where(reached, a, b), new, before)

    return lax.fori_loop(0, length, step, start)


def chain_join(earlier, following):
    return (earlier[0] * following[0], following[0][:, None, None] * earlier[1] + following[1])


def causal_filter(stream_rows, previous, kernel_taps):
    rim_rows = previous.shape[0]
    length = stream_rows.shape[0]
    extended = jnp.concatenate([previous, stream_rows], axis=0).astype(jnp.float32)
    result = jnp.zeros(stream_rows.shape, jnp.float32)
    for offset in range(kernel_taps.shape[0]):
        result = (
            result + kernel_taps[offset] * extended[rim_rows - offset : rim_rows - offset + length]
        )
    return result


def filter_back(post_rows, following_rows, kernel_taps):
    length = post_rows.shape[0]
    extended = jnp.concatenate([post_rows, following_rows], axis=0)
    result = jnp.zeros(post_rows.shape, jnp.float32)
    for offset in range(kernel_taps.shape[0]):
        result = result + kernel_taps[offset] * extended[offset : offset + length]
    return result


def tap_sums(post_rows, stream_rows, previous, kernel_width):
    rim_rows = previous.shape[0]
    length = stream_rows.shape[0]
    extended = jnp.concatenate([previous, stream_rows], axis=0).astype(jnp.float32)
    return jnp.stack(
        [
            jnp.sum(post_rows * extended[rim_rows - offset : rim_rows - offset + length], axis=0)
            for offset in range(kernel_width)
        ]
    )


def local(activations, value_weight, query_in, key_in, grad_out, conv_kernel, log_gate):
    tok_rows = query_in.shape[1]
    channels = query_in.shape[2]
    head_count = log_gate.shape[1]
    head_size = channels // head_count
    kernel_width = conv_kernel.shape[1]
    rim_rows = kernel_width - 1
    grad_scale = 1.0 / math.sqrt(lax.axis_size("seq") * lax.axis_size("rep") * tok_rows)
    query_rows = query_in[0]
    key_rows = key_in[0]
    gathered = lax.all_gather(activations, "head", axis=2, tiled=True)[0]
    columns = gathered
    value_f32 = jnp.dot(
        columns,
        lax.all_gather(value_weight, ("seq", "rep"), axis=0, tiled=True),
        preferred_element_type=jnp.float32,
    )
    value_raw = value_f32.astype(jnp.bfloat16)
    before_all = shifted(
        jnp.stack(
            [
                query_rows[tok_rows - rim_rows :],
                key_rows[tok_rows - rim_rows :],
                value_raw[tok_rows - rim_rows :],
            ]
        ),
        "seq",
        1,
    )
    before = (before_all[0], before_all[1], before_all[2])
    raw_rows = (query_rows, key_rows, value_raw)
    convolved = [
        causal_filter(raw_rows[which], before[which], conv_kernel[which]).astype(jnp.bfloat16)
        for which in range(3)
    ]
    query_heads = convolved[0].reshape(tok_rows, head_count, head_size)
    key_heads = convolved[1].reshape(tok_rows, head_count, head_size)
    value_heads = convolved[2].reshape(tok_rows, head_count, head_size)
    cumulative = jnp.cumsum(log_gate[0], axis=1)
    final_cum = cumulative[:, -1]
    block_decay = jnp.exp(final_cum)
    rising = jnp.exp(cumulative).T[:, :, None]
    shrink = jnp.exp(final_cum[:, None] - cumulative).T[:, :, None]
    mixing = jnp.exp(-jnp.abs(cumulative[:, :, None] - cumulative[:, None, :]))
    scores = (
        mixing
        * jnp.einsum("thd,shd->hts", query_heads, key_heads, preferred_element_type=jnp.float32)
    ).astype(jnp.bfloat16)
    fwd_sum = jnp.einsum(
        "thd,the->hde",
        (shrink * key_heads).astype(jnp.bfloat16),
        value_heads,
        preferred_element_type=jnp.float32,
    )
    back_sum = jnp.einsum(
        "thd,the->hde",
        (rising * key_heads).astype(jnp.bfloat16),
        value_heads,
        preferred_element_type=jnp.float32,
    )
    identity = (
        jnp.ones((head_count,), jnp.float32),
        jnp.zeros((head_count, head_size, head_size), jnp.float32),
    )
    left_b = prefix((block_decay, fwd_sum), "seq", chain_join, identity, False)[1].astype(
        jnp.bfloat16
    )
    right_b = prefix((block_decay, back_sum), "seq", chain_join, identity, True)[1].astype(
        jnp.bfloat16
    )
    attn = rising * jnp.einsum(
        "thd,hde->the", query_heads, left_b, preferred_element_type=jnp.float32
    )
    attn = attn + shrink * jnp.einsum(
        "thd,hde->the", query_heads, right_b, preferred_element_type=jnp.float32
    )
    attn = attn + jnp.einsum(
        "hts,she->the", scores, value_heads, preferred_element_type=jnp.float32
    )
    root_mean = jnp.sqrt(jnp.mean(attn * attn, axis=2, keepdims=True) + EPSILON)
    normed = attn / root_mean
    attn_out = normed.astype(jnp.bfloat16).reshape(1, tok_rows, channels)
    upstream = grad_out[0].reshape(tok_rows, head_count, head_size).astype(jnp.float32)
    grad_attn = (
        (upstream - normed * jnp.mean(upstream * normed, axis=2, keepdims=True)) / root_mean
    ).astype(jnp.bfloat16)
    grad_scores = (
        mixing
        * jnp.einsum("the,she->hts", grad_attn, value_heads, preferred_element_type=jnp.float32)
    ).astype(jnp.bfloat16)
    fwd_grad = jnp.einsum(
        "thd,the->hde",
        (shrink * query_heads).astype(jnp.bfloat16),
        grad_attn,
        preferred_element_type=jnp.float32,
    )
    back_grad = jnp.einsum(
        "thd,the->hde",
        (rising * query_heads).astype(jnp.bfloat16),
        grad_attn,
        preferred_element_type=jnp.float32,
    )
    left_gb = carried_in((block_decay, fwd_grad), "seq", chain_join, identity, False)[1].astype(
        jnp.bfloat16
    )
    right_gb = carried_in((block_decay, back_grad), "seq", chain_join, identity, True)[1].astype(
        jnp.bfloat16
    )
    query_post = rising * jnp.einsum(
        "the,hde->thd", grad_attn, left_b, preferred_element_type=jnp.float32
    )
    query_post = query_post + shrink * jnp.einsum(
        "the,hde->thd", grad_attn, right_b, preferred_element_type=jnp.float32
    )
    query_post = query_post + jnp.einsum(
        "hts,shd->thd", grad_scores, key_heads, preferred_element_type=jnp.float32
    )
    key_post = rising * jnp.einsum(
        "the,hde->thd", value_heads, left_gb, preferred_element_type=jnp.float32
    )
    key_post = key_post + shrink * jnp.einsum(
        "the,hde->thd", value_heads, right_gb, preferred_element_type=jnp.float32
    )
    key_post = key_post + jnp.einsum(
        "hts,thd->shd", grad_scores, query_heads, preferred_element_type=jnp.float32
    )
    value_post = rising * jnp.einsum(
        "thd,hde->the", key_heads, left_gb, preferred_element_type=jnp.float32
    )
    value_post = value_post + shrink * jnp.einsum(
        "thd,hde->the", key_heads, right_gb, preferred_element_type=jnp.float32
    )
    value_post = value_post + jnp.einsum(
        "hts,the->she", scores, grad_attn, preferred_element_type=jnp.float32
    )
    post_grads = jnp.stack(
        [
            query_post.reshape(tok_rows, channels),
            key_post.reshape(tok_rows, channels),
            value_post.reshape(tok_rows, channels),
        ]
    )
    following = shifted(post_grads[:, :rim_rows].astype(jnp.bfloat16), "seq", -1).astype(
        jnp.float32
    )
    grad_query = filter_back(post_grads[0], following[0], conv_kernel[0]).astype(jnp.bfloat16)
    grad_key = filter_back(post_grads[1], following[1], conv_kernel[1]).astype(jnp.bfloat16)
    grad_value = filter_back(post_grads[2], following[2], conv_kernel[2]).astype(jnp.bfloat16)
    kernel_terms = (
        jnp.stack(
            [
                tap_sums(post_grads[which], raw_rows[which], before[which], kernel_width)
                for which in range(3)
            ]
        )
        * grad_scale
    )
    grad_conv = lax.psum(kernel_terms, ("seq", "rep"))
    partial_x = lax.dot_general(
        grad_value,
        lax.all_gather(value_weight, ("seq", "rep"), axis=0, tiled=True),
        (((1,), (1,)), ((), ())),
        preferred_element_type=jnp.float32,
    )
    grad_x = lax.psum_scatter(
        partial_x[None].astype(jnp.bfloat16), "head", scatter_dimension=2, tiled=True
    )
    columns = gathered
    grad_w = lax.psum_scatter(
        lax.dot_general(
            columns, grad_value, (((0,), (0,)), ((), ())), preferred_element_type=jnp.float32
        )
        * grad_scale,
        ("seq", "rep"),
        scatter_dimension=0,
        tiled=True,
    )
    return (attn_out, grad_query[None], grad_key[None], grad_x, grad_w, grad_conv)


def solution(mesh):
    placed = (
        P(("parts", "rep"), "seq", "head"),
        P(("seq", "rep"), "head"),
        P(("parts", "rep"), "seq", "head"),
        P(("parts", "rep"), "seq", "head"),
        P(("parts", "rep"), "seq", "head"),
        P(None, None, "head"),
        P(("parts", "rep"), "head", "seq"),
    )
    return jax.shard_map(
        local,
        mesh=mesh,
        in_specs=placed,
        out_specs=(
            P(("parts", "rep"), "seq", "head"),
            P(("parts", "rep"), "seq", "head"),
            P(("parts", "rep"), "seq", "head"),
            P(("parts", "rep"), "seq", "head"),
            P(("parts", "seq", "rep"), "head"),
            P("parts", None, "head"),
        ),
        check_vma=False,
    )
```

profile of v0, /device:TPU:0, one launch (start us, length us, event | category | flops | bytes accessed | tf_op | source)
XLA Modules:
  0.0 710.2 jit_solution(15877381056896727067)
XLA Ops:
  11.9 75.4 %all-gather.12.cloned.1.call-done = bf16[2048,2048]{1,0:T(8,128)(2,1)} async-done(((bf16[128,2048]{1,0:T(8,128)(2,1)}), bf16[2048,2048]{1,0:T(8,128)(2,1)}) %all-gather.12.cloned.1.call-update) | async-done | bytes 8388624 | tf_op jit(solution)/shard_map/all_gather | solution.py:107
  87.2 4.6 convolution_convert_fusion.1
  105.4 16.3 %all-reduce = f32[128]{0:T(128)S(1)} all-reduce(f32[128]{0:T(128)S(1)} %dynamic-update-slice), channel_id=2, replica_groups=mesh['parts'=2,'seq'=8,'rep'=2,'head'=1] {'seq'}, use_global_device_ids=true, to_apply=%add | all-reduce | flops 128 | bytes 1024
  127.9 54.5 %all-gather.14.cloned.1.call-done = f32[128,128,128]{2,1,0:T(8,128)} async-done(((f32[16,128,128]{2,1,0:T(8,128)}), f32[128,128,128]{2,1,0:T(8,128)}) %all-gather.14.cloned.1.call-update) | async-done | bytes 8388624 | tf_op jit(solution)/shard_map/all_gather | solution.py:20
  183.5 2.6 fusion.18
  186.2 78.5 %all-gather.16.cloned.1.call-done = f32[128,128,128]{2,1,0:T(8,128)} async-done(((f32[16,128,128]{2,1,0:T(8,128)}), f32[128,128,128]{2,1,0:T(8,128)}) %all-gather.16.cloned.1.call-update) | async-done | bytes 8388624 | tf_op jit(solution)/shard_map/all_gather | solution.py:20
  265.8 18.6 %while.57 = (s32[]{:T(128)}, f32[16,128,128]{2,1,0:T(8,128)}, s32[]{:T(128)}, f32[8,16]{1,0:T(8,128)S(1)}, f32[8,16,128,128]{3,2,1,0:T(8,128)}, /*index=5*/s32[]{:T(128)}, s32[]{:T(128)}, s32[]{:T(128)}, s32[]{:T(128)}) while((s32[]{:T(128)}, f32[16,128,128]{2,1,0:T(8,128)}, s32[]{:T(128)}, f32[8,16]{1,0:T(8,128)S(1)}, ...), condition=%wide.region_4.5_spmd, body=%wide.region_3.4_spmd.sunk | while | flops 524294 | bytes 3146075 | solution.py:29
  265.8 2.7 bitcast_add_fusion.5
  268.4 2.7 bitcast_add_fusion.5
  271.1 2.7 bitcast_add_fusion.5
  273.8 2.7 bitcast_add_fusion.5
  276.4 2.7 bitcast_add_fusion.5
  279.1 2.7 bitcast_add_fusion.5
  281.7 2.7 bitcast_add_fusion.5
  293.9 14.5 %all-reduce.1 = bf16[128]{0:T(256)(128)(2,1)S(1)} all-reduce(bf16[128]{0:T(256)(128)(2,1)S(1)} %dynamic-update-slice.1), channel_id=7, replica_groups=mesh['parts'=2,'seq'=8,'rep'=2,'head'=1] {'seq'}, use_global_device_ids=true, to_apply=%add.1 | all-reduce | flops 128 | bytes 512
  316.6 19.6 %all-gather.18.cloned.1.call-done = bf16[128,128,128]{2,1,0:T(8,128)(2,1)} async-done(((bf16[16,128,128]{2,1,0:T(8,128)(2,1)}), bf16[128,128,128]{2,1,0:T(8,128)(2,1)}) %all-gather.18.cloned.1.call-update) | async-done | bytes 4194320 | tf_op jit(solution)/shard_map/all_gather | solution.py:35
  336.2 20.2 %while.58 = (s32[]{:T(128)}, f32[16,128,128]{2,1,0:T(8,128)}, s32[]{:T(128)}, bf16[8,16]{1,0:T(8,128)(2,1)S(1)}, bf16[8,16,128,128]{3,2,1,0:T(8,128)(2,1)}, /*index=5*/s32[]{:T(128)}, s32[]{:T(128)}) while((s32[]{:T(128)}, f32[16,128,128]{2,1,0:T(8,128)}, s32[]{:T(128)}, bf16[8,16]{1,0:T(8,128)(2,1)S(1)}, ...), condition=%wide.region_8.9_spmd.clone, body=%wide.region_7.8_spmd.clone.sunk | while | flops 1310740 | bytes 2621713 | solution.py:53
  356.4 2.8 fusion.6
  360.7 22.6 %all-gather.20.cloned.1.call-done = bf16[128,128,128]{2,1,0:T(8,128)(2,1)} async-done(((bf16[16,128,128]{2,1,0:T(8,128)(2,1)}), bf16[128,128,128]{2,1,0:T(8,128)(2,1)}) %all-gather.20.cloned.1.call-update) | async-done | bytes 4194320 | tf_op jit(solution)/shard_map/all_gather | solution.py:35
  383.4 20.9 %while.59 = (s32[]{:T(128)}, f32[16,128,128]{2,1,0:T(8,128)}, s32[]{:T(128)}, bf16[8,16]{1,0:T(8,128)(2,1)S(1)}, bf16[8,16,128,128]{3,2,1,0:T(8,128)(2,1)}, /*index=5*/s32[]{:T(128)}, s32[]{:T(128)}, s32[]{:T(128)}, s32[]{:T(128)}) while((s32[]{:T(128)}, f32[16,128,128]{2,1,0:T(8,128)}, s32[]{:T(128)}, ...), condition=%wide.region_10.11_spmd.clone, body=%wide.region_9.10_spmd.clone.sunk | while | flops 1310744 | bytes 2621775 | solution.py:53
  385.7 2.6 fusion.120
  388.3 2.6 fusion.120
  391.0 2.6 fusion.120
  393.6 2.6 fusion.120
  396.3 2.6 fusion.120
  398.9 2.6 fusion.120
  420.3 3.6 multiply_reduce_fusion.3
  423.9 8.1 %multiply_bitcast_fusion = f32[2048,2048]{0,1:T(8,128)} fusion(bf16[128,2048]{1,0:T(8,128)(2,1)S(1)} %get-tuple-element.476, bf16[1,128,2048]{2,1,0:T(8,128)(2,1)S(1)} %copy-done), kind=kOutput, calls=%fused_computation.10 | convolution fusion | flops 1077936128 | bytes 17825792 | tf_op jit(solution)/shard_map/dot_general | solution.py:262
  438.3 4.3 multiply_reduce_fusion.7
  445.1 8.5 %fusion.2 = bf16[1,128,2048]{2,1,0:T(8,128)(2,1)} fusion(bf16[128,2048]{1,0:T(8,128)(2,1)S(1)} %get-tuple-element.476, bf16[2048,2048]{1,0:T(8,128)(2,1)} %all-gather.12.cloned.1.call-done), kind=kOutput, calls=%fused_computation.13 | convolution fusion | flops 1074003968 | bytes 9437184 | tf_op jit(solution)/shard_map/dot_general | solution.py:251
  453.6 156.4 %reduce-scatter.2.cloned.1.call-done = f32[128,2048]{0,1:T(8,128)} async-done(((f32[2048,2048]{0,1:T(8,128)}), f32[128,2048]{0,1:T(8,128)}) %reduce-scatter.2.cloned.1.call-update) | async-done | bytes 1048592 | tf_op jit(solution)/shard_map/reduce_scatter | solution.py:261
  612.5 89.3 %all-reduce.4.cloned.1.call-done = f32[3,4,2048]{2,1,0:T(4,128)} async-done(((f32[3,4,2048]{2,1,0:T(4,128)}), f32[3,4,2048]{2,1,0:T(4,128)}) %all-reduce.4.cloned.1.call-update) | async-done | bytes 98320 | tf_op jit(solution)/shard_map/psum | solution.py:250
  (168 shorter events, 98.9 us)
Async XLA Ops:
  7.2 80.1 %copy-start = (bf16[1,128,2048]{2,1,0:T(8,128)(2,1)S(1)}, bf16[1,128,2048]{2,1,0:T(8,128)(2,1)}, u32[]{:S(2)}) copy-start(bf16[1,128,2048]{2,1,0:T(8,128)(2,1)} %param.15) | copy-start | bytes 1572868
  7.2 80.1 %all-gather.12.cloned.1.call-start = ((), (), s32[]{:S(2)}) async-start(), calls=%async_computation.1 | async-start | bytes 8912896 | tf_op jit(solution)/shard_map/all_gather | solution.py:107
  7.9 174.5 %all-gather.14.cloned.1.call-start = ((), (), s32[]{:S(2)}) async-start(), calls=%async_computation.4 | async-start | bytes 9437184 | tf_op jit(solution)/shard_map/all_gather | solution.py:20
  11.9 83.1 %copy-start.22 = (bf16[1,128,2048]{2,1,0:T(8,128)(2,1)S(1)}, bf16[1,128,2048]{2,1,0:T(8,128)(2,1)}, u32[]{:S(2)}) copy-start(bf16[1,128,2048]{2,1,0:T(8,128)(2,1)} %param.18) | copy-start | bytes 1572868
  92.0 3.0 collective-permute-start
  97.3 1.9 copy-start.9
  99.2 165.5 %all-gather.16.cloned.1.call-start = ((), (), s32[]{:S(2)}) async-start(), calls=%async_computation.5 | async-start | bytes 9437184 | tf_op jit(solution)/shard_map/all_gather | solution.py:20
  101.5 2.4 copy-start.24
  101.5 20.2 %copy-start.23 = (bf16[1,128,2048]{2,1,0:T(8,128)(2,1)S(1)}, bf16[1,128,2048]{2,1,0:T(8,128)(2,1)}, u32[]{:S(2)}) copy-start(bf16[1,128,2048]{2,1,0:T(8,128)(2,1)} %param.17) | copy-start | bytes 1572868
  101.6 234.7 %all-gather.18.cloned.1.call-start = ((), (), s32[]{:S(2)}) async-start(), calls=%async_computation.6 | async-start | bytes 4718592 | tf_op jit(solution)/shard_map/all_gather | solution.py:35
  121.9 1.1 copy-start.1
  284.4 2.0 copy-start.10
  284.4 2.0 copy-start.20
  286.4 1.2 copy-start.14
  290.9 92.4 %all-gather.20.cloned.1.call-start = ((), (), s32[]{:S(2)}) async-start(), calls=%async_computation.7 | async-start | bytes 4718592 | tf_op jit(solution)/shard_map/all_gather | solution.py:35
  293.3 316.7 %reduce-scatter.2.cloned.1.call-start = ((), (), s32[]{:S(2)}) async-start(), calls=%async_computation.2 | async-start | bytes 17825792 | tf_op jit(solution)/shard_map/reduce_scatter | solution.py:261
  308.5 1.9 copy-start.4
  308.5 1.9 copy-start.7
  310.4 1.7 copy-start.17
  310.4 1.4 copy-start.3
  311.9 1.0 copy-start.13
  356.4 2.8 copy-start.5
  356.4 2.8 copy-start.11
  404.2 2.1 copy-start.8
  404.2 2.2 copy-start.21
  409.9 2.2 copy-start.18
  413.5 2.1 copy-start.19
  416.4 3.9 collective-permute-start.1
  432.0 2.4 copy-start.15
  432.0 269.8 %all-reduce.4.cloned.1.call-start = ((), (), s32[]{:S(2)}) async-start(), calls=%async_computation.3 | async-start | bytes 196608 | tf_op jit(solution)/shard_map/psum | solution.py:250
  438.3 4.3 copy-start.2
  438.3 4.3 copy-start.16
  (2 other events, 1.8 us)
Sparse Core Ops, SparseCore 0:
  10.2 76.9 all-gather.11
  99.3 83.1 all-gather.13
  184.1 80.5 all-gather.15
  291.1 45.1 all-gather.17
  337.7 45.6 all-gather.19
  432.1 177.8 reduce-scatter.1
  614.0 87.7 all-reduce.3
where the time goes:
time: 712 us; the launch traced here: 710 us
  waiting for transfers between devices  498 us (70%)
  other arithmetic  75.9 us (11%)
  matrix products  51.7 us (7%)
  local copies, waits for them, and re-layouts  34.8 us (5%)
  blocking collectives  30.8 us (4%)
  between operations  15.2 us (2%)
    reduce_scatter x1, waiting for transfers between devices, local(): lax.psum_scatter(lax.dot_general(columns, grad_value, (((0,), (0,)), ((),...  156 us
    all_gather x2, waiting for transfers between devices, prefix(): gathered = jax.tree.map(lambda a: lax.all_gather(a, axis), part)  133 us
    psum x1, waiting for transfers between devices, local(): grad_conv = lax.psum(kernel_terms, ('seq', 'rep'))  89.3 us
    all_gather x1, waiting for transfers between devices, local(): lax.all_gather(value_weight, ('seq', 'rep'), axis=0, tiled=True)  75.4 us
    all_gather x2, waiting for transfers between devices, carried_in(): lax.all_gather(part.astype(kind), axis)  42.3 us
    select_n x16, other arithmetic, step(): return jax.tree.map(lambda a, b: jnp.where(reached, a, b), new, before)  40.9 us
    unnamed x2, blocking collectives  30.8 us
    add x7, other arithmetic, chain_join(): following[0][:, None, None] * earlier[1] + following[1]  18.6 us
  transfers between devices with their start and end apart: 9, of which 8 were waited for; matrix products, arithmetic and copies ran while one was open for 11% of the time, Pallas kernels for 0%

commit v1 on v0

--- a/solution.py
+++ b/solution.py
@@ -247,7 +247,8 @@
         )
         * grad_scale
     )
-    grad_conv = lax.psum(kernel_terms, ("seq", "rep"))
+    field_out = lax.all_gather(kernel_terms, ("seq", "rep"))
+    grad_conv = jnp.sum(field_out, axis=0)
     partial_x = lax.dot_general(
         grad_value,
         lax.all_gather(value_weight, ("seq", "rep"), axis=0, tiled=True),

time: 712 us -> 667 us (0.937)
  waiting for transfers between devices: 498 us -> 453 us
    psum x1 -> x0, waiting for transfers between devices: 89.3 us -> none  [local(): grad_conv = lax.psum(kernel_terms, ('seq', 'rep'))]
    all_gather x0 -> x1, waiting for transfers between devices: none -> 23 us  [local(): field_out = lax.all_gather(kernel_terms, ('seq', 'rep'))]
    reduce_scatter x1, waiting for transfers between devices: 156 us -> 178 us  [local(): lax.psum_scatter(lax.dot_general(columns, grad_value, (((0,), (0,)), ((),...]
  transfers between devices with their start and end apart: 9 -> 9, of which waited for: 8 -> 8; matrix products, arithmetic and copies ran while one was open for 11% -> 12% of each run, Pallas kernels for 0% -> 0%
where the time goes in v1:
time: 667 us; the launch traced here: 665 us
  waiting for transfers between devices  453 us (68%)
  other arithmetic  77.1 us (12%)
  matrix products  50.3 us (8%)
  local copies, waits for them, and re-layouts  34.4 us (5%)
  blocking collectives  30.9 us (5%)
  between operations  15.2 us (2%)
    reduce_scatter x1, waiting for transfers between devices, local(): lax.psum_scatter(lax.dot_general(columns, grad_value, (((0,), (0,)), ((),...  178 us
    all_gather x2, waiting for transfers between devices, prefix(): gathered = jax.tree.map(lambda a: lax.all_gather(a, axis), part)  133 us
    all_gather x1, waiting for transfers between devices, local(): lax.all_gather(value_weight, ('seq', 'rep'), axis=0, tiled=True)  75.4 us
    all_gather x2, waiting for transfers between devices, carried_in(): lax.all_gather(part.astype(kind), axis)  42.2 us
    select_n x16, other arithmetic, step(): return jax.tree.map(lambda a, b: jnp.where(reached, a, b), new, before)  40.9 us
    unnamed x2, blocking collectives  30.9 us
    all_gather x1, waiting for transfers between devices, local(): field_out = lax.all_gather(kernel_terms, ('seq', 'rep'))  23 us
    add x7, other arithmetic, chain_join(): following[0][:, None, None] * earlier[1] + following[1]  18.6 us
  transfers between devices with their start and end apart: 9, of which 8 were waited for; matrix products, arithmetic and copies ran while one was open for 12% of the time, Pallas kernels for 0%

profile of v1, /device:TPU:0, one launch (start us, length us, event | category | flops | bytes accessed | tf_op | source)
XLA Modules:
  0.0 664.7 jit_solution(7994802415581432285)
XLA Ops:
  11.9 75.4 %all-gather.13.cloned.1.call-done = bf16[2048,2048]{1,0:T(8,128)(2,1)} async-done(((bf16[128,2048]{1,0:T(8,128)(2,1)}), bf16[2048,2048]{1,0:T(8,128)(2,1)}) %all-gather.13.cloned.1.call-update) | async-done | bytes 8388624 | tf_op jit(solution)/shard_map/all_gather | solution.py:107
  87.2 4.6 convolution_convert_fusion.1
  105.4 16.3 %all-reduce = f32[128]{0:T(128)S(1)} all-reduce(f32[128]{0:T(128)S(1)} %dynamic-update-slice), channel_id=2, replica_groups=mesh['parts'=2,'seq'=8,'rep'=2,'head'=1] {'seq'}, use_global_device_ids=true, to_apply=%add | all-reduce | flops 128 | bytes 1024
  127.9 54.5 %all-gather.17.cloned.1.call-done = f32[128,128,128]{2,1,0:T(8,128)} async-done(((f32[16,128,128]{2,1,0:T(8,128)}), f32[128,128,128]{2,1,0:T(8,128)}) %all-gather.17.cloned.1.call-update) | async-done | bytes 8388624 | tf_op jit(solution)/shard_map/all_gather | solution.py:20
  183.5 2.6 fusion.18
  186.2 78.5 %all-gather.19.cloned.1.call-done = f32[128,128,128]{2,1,0:T(8,128)} async-done(((f32[16,128,128]{2,1,0:T(8,128)}), f32[128,128,128]{2,1,0:T(8,128)}) %all-gather.19.cloned.1.call-update) | async-done | bytes 8388624 | tf_op jit(solution)/shard_map/all_gather | solution.py:20
  265.8 18.6 %while.57 = (s32[]{:T(128)}, f32[16,128,128]{2,1,0:T(8,128)}, s32[]{:T(128)}, f32[8,16]{1,0:T(8,128)S(1)}, f32[8,16,128,128]{3,2,1,0:T(8,128)}, /*index=5*/s32[]{:T(128)}, s32[]{:T(128)}, s32[]{:T(128)}, s32[]{:T(128)}) while((s32[]{:T(128)}, f32[16,128,128]{2,1,0:T(8,128)}, s32[]{:T(128)}, f32[8,16]{1,0:T(8,128)S(1)}, ...), condition=%wide.region_4.5_spmd, body=%wide.region_3.4_spmd.sunk | while | flops 524294 | bytes 3146075 | solution.py:29
  265.8 2.7 bitcast_add_fusion.5
  268.4 2.7 bitcast_add_fusion.5
  271.1 2.7 bitcast_add_fusion.5
  273.8 2.7 bitcast_add_fusion.5
  276.4 2.7 bitcast_add_fusion.5
  279.1 2.7 bitcast_add_fusion.5
  281.7 2.7 bitcast_add_fusion.5
  293.9 14.6 %all-reduce.1 = bf16[128]{0:T(256)(128)(2,1)S(1)} all-reduce(bf16[128]{0:T(256)(128)(2,1)S(1)} %dynamic-update-slice.1), channel_id=7, replica_groups=mesh['parts'=2,'seq'=8,'rep'=2,'head'=1] {'seq'}, use_global_device_ids=true, to_apply=%add.1 | all-reduce | flops 128 | bytes 512
  316.8 19.5 %all-gather.21.cloned.1.call-done = bf16[128,128,128]{2,1,0:T(8,128)(2,1)} async-done(((bf16[16,128,128]{2,1,0:T(8,128)(2,1)}), bf16[128,128,128]{2,1,0:T(8,128)(2,1)}) %all-gather.21.cloned.1.call-update) | async-done | bytes 4194320 | tf_op jit(solution)/shard_map/all_gather | solution.py:35
  336.3 20.2 %while.58 = (s32[]{:T(128)}, f32[16,128,128]{2,1,0:T(8,128)}, s32[]{:T(128)}, bf16[8,16]{1,0:T(8,128)(2,1)S(1)}, bf16[8,16,128,128]{3,2,1,0:T(8,128)(2,1)}, /*index=5*/s32[]{:T(128)}, s32[]{:T(128)}) while((s32[]{:T(128)}, f32[16,128,128]{2,1,0:T(8,128)}, s32[]{:T(128)}, bf16[8,16]{1,0:T(8,128)(2,1)S(1)}, ...), condition=%wide.region_8.9_spmd.clone, body=%wide.region_7.8_spmd.clone.sunk | while | flops 1310740 | bytes 2621713 | solution.py:53
  356.5 2.8 fusion.6
  360.8 22.6 %all-gather.23.cloned.1.call-done = bf16[128,128,128]{2,1,0:T(8,128)(2,1)} async-done(((bf16[16,128,128]{2,1,0:T(8,128)(2,1)}), bf16[128,128,128]{2,1,0:T(8,128)(2,1)}) %all-gather.23.cloned.1.call-update) | async-done | bytes 4194320 | tf_op jit(solution)/shard_map/all_gather | solution.py:35
  383.4 20.9 %while.59 = (s32[]{:T(128)}, f32[16,128,128]{2,1,0:T(8,128)}, s32[]{:T(128)}, bf16[8,16]{1,0:T(8,128)(2,1)S(1)}, bf16[8,16,128,128]{3,2,1,0:T(8,128)(2,1)}, /*index=5*/s32[]{:T(128)}, s32[]{:T(128)}, s32[]{:T(128)}, s32[]{:T(128)}) while((s32[]{:T(128)}, f32[16,128,128]{2,1,0:T(8,128)}, s32[]{:T(128)}, ...), condition=%wide.region_10.11_spmd.clone, body=%wide.region_9.10_spmd.clone.sunk | while | flops 1310744 | bytes 2621775 | solution.py:53
  385.8 2.6 fusion.120
  388.4 2.6 fusion.120
  391.1 2.6 fusion.120
  393.7 2.6 fusion.120
  396.4 2.6 fusion.120
  399.0 2.6 fusion.120
  401.7 2.6 fusion.120
  425.6 5.6 multiply_reduce_fusion.11
  435.0 8.1 %multiply_bitcast_fusion = f32[2048,2048]{0,1:T(8,128)} fusion(bf16[128,2048]{1,0:T(8,128)(2,1)S(1)} %get-tuple-element.476, bf16[1,128,2048]{2,1,0:T(8,128)(2,1)S(1)} %copy-done), kind=kOutput, calls=%fused_computation.10 | convolution fusion | flops 1077936128 | bytes 17825792 | tf_op jit(solution)/shard_map/dot_general | solution.py:263
  445.2 7.1 %fusion.2 = bf16[1,128,2048]{2,1,0:T(8,128)(2,1)} fusion(bf16[128,2048]{1,0:T(8,128)(2,1)S(1)} %get-tuple-element.476, bf16[2048,2048]{1,0:T(8,128)(2,1)} %all-gather.13.cloned.1.call-done), kind=kOutput, calls=%fused_computation.13 | convolution fusion | flops 1074003968 | bytes 9437184 | tf_op jit(solution)/shard_map/dot_general | solution.py:252
  452.2 23.0 %all-gather.15.cloned.1.call-done = f32[16,3,4,2048]{3,2,1,0:T(4,128)} async-done(((f32[1,3,4,2048]{3,2,1,0:T(4,128)}), f32[16,3,4,2048]{3,2,1,0:T(4,128)}) %all-gather.15.cloned.1.call-update) | async-done | bytes 1572880 | tf_op jit(solution)/shard_map/all_gather | solution.py:250
  477.6 177.6 %reduce-scatter.2.cloned.1.call-done = f32[128,2048]{0,1:T(8,128)} async-done(((f32[2048,2048]{0,1:T(8,128)}), f32[128,2048]{0,1:T(8,128)}) %reduce-scatter.2.cloned.1.call-update) | async-done | bytes 1048592 | tf_op jit(solution)/shard_map/reduce_scatter | solution.py:262
  (168 shorter events, 99.4 us)
Async XLA Ops:
  7.2 80.1 %copy-start = (bf16[1,128,2048]{2,1,0:T(8,128)(2,1)S(1)}, bf16[1,128,2048]{2,1,0:T(8,128)(2,1)}, u32[]{:S(2)}) copy-start(bf16[1,128,2048]{2,1,0:T(8,128)(2,1)} %param.15) | copy-start | bytes 1572868
  7.2 80.1 %all-gather.13.cloned.1.call-start = ((), (), s32[]{:S(2)}) async-start(), calls=%async_computation.1 | async-start | bytes 8912896 | tf_op jit(solution)/shard_map/all_gather | solution.py:107
  7.9 174.5 %all-gather.17.cloned.1.call-start = ((), (), s32[]{:S(2)}) async-start(), calls=%async_computation.4 | async-start | bytes 9437184 | tf_op jit(solution)/shard_map/all_gather | solution.py:20
  11.9 83.2 %copy-start.22 = (bf16[1,128,2048]{2,1,0:T(8,128)(2,1)S(1)}, bf16[1,128,2048]{2,1,0:T(8,128)(2,1)}, u32[]{:S(2)}) copy-start(bf16[1,128,2048]{2,1,0:T(8,128)(2,1)} %param.18) | copy-start | bytes 1572868
  92.0 3.0 collective-permute-start
  96.8 1.0 copy-start.11
  97.3 1.9 copy-start.8
  99.2 165.5 %all-gather.19.cloned.1.call-start = ((), (), s32[]{:S(2)}) async-start(), calls=%async_computation.5 | async-start | bytes 9437184 | tf_op jit(solution)/shard_map/all_gather | solution.py:20
  101.5 2.4 copy-start.24
  101.5 20.2 %copy-start.23 = (bf16[1,128,2048]{2,1,0:T(8,128)(2,1)S(1)}, bf16[1,128,2048]{2,1,0:T(8,128)(2,1)}, u32[]{:S(2)}) copy-start(bf16[1,128,2048]{2,1,0:T(8,128)(2,1)} %param.17) | copy-start | bytes 1572868
  101.6 234.8 %all-gather.21.cloned.1.call-start = ((), (), s32[]{:S(2)}) async-start(), calls=%async_computation.6 | async-start | bytes 4718592 | tf_op jit(solution)/shard_map/all_gather | solution.py:35
  121.9 1.1 copy-start.1
  284.4 2.0 copy-start.9
  284.4 2.0 copy-start.19
  286.4 1.2 copy-start.13
  291.0 92.4 %all-gather.23.cloned.1.call-start = ((), (), s32[]{:S(2)}) async-start(), calls=%async_computation.7 | async-start | bytes 4718592 | tf_op jit(solution)/shard_map/all_gather | solution.py:35
  293.4 181.9 %all-gather.15.cloned.1.call-start = ((), (), s32[]{:S(2)}) async-start(), calls=%async_computation.3 | async-start | bytes 1671168 | tf_op jit(solution)/shard_map/all_gather | solution.py:250
  308.7 1.9 copy-start.2
  308.7 1.9 copy-start.6
  310.6 1.7 copy-start.16
  310.6 1.4 copy-start.3
  356.5 2.8 copy-start.4
  356.5 2.8 copy-start.10
  404.3 2.1 copy-start.7
  404.3 2.2 copy-start.20
  409.9 2.2 copy-start.17
  413.6 2.1 copy-start.18
  416.5 9.0 %collective-permute-start.1 = (bf16[3,3,2048]{2,1,0:T(4,128)(2,1)S(1)}, bf16[3,3,2048]{2,1,0:T(4,128)(2,1)S(1)}, u32[]{:S(2)}, u32[]{:S(2)}) collective-permute-start(bf16[3,3,2048]{2,1,0:T(4,128)(2,1)S(1)} %pad_maximum_fusion.3), channel_id=1, source_target_pairs={{2,0},{4,2},{6,4},{8,6},{10,8},{12,10},{14,12},{3,1},{5,3},{7,5},{... | collective-permute-start | bytes 110600 | tf_op jit(solution)/shard_map/ppermute | solution.py:13
  425.5 5.6 copy-start.15
  431.2 1.7 copy-start.14
  434.8 220.5 %reduce-scatter.2.cloned.1.call-start = ((), (), s32[]{:S(2)}) async-start(), calls=%async_computation.2 | async-start | bytes 17825792 | tf_op jit(solution)/shard_map/reduce_scatter | solution.py:262
  443.1 1.0 copy-start.21
  (2 other events, 1.9 us)
Sparse Core Ops, SparseCore 0:
  10.2 76.9 all-gather.12
  99.3 83.1 all-gather.16
  184.1 80.5 all-gather.18
  291.1 45.1 all-gather.20
  337.8 45.6 all-gather.22
  434.9 40.3 all-gather.14
  479.4 175.8 reduce-scatter.1
